TPU v7x, 256 devices: a whole 4x4x8 slice. The times are simulated.
256 devices in a mesh: cfg: 2 (over x_lo), seq: 128 (over y, z, x_hi, core).
Axes of the slice: x: 4 (x_hi: 2, x_lo: 2; x = x_hi * 2 + x_lo), y: 4, z: 8, core: 2. Of those that a mesh axis runs over, the one named last changes fastest.
Arguments:
- queries: bfloat16 [2, 4608, 1536], P('cfg', 'seq'), may hold values from -25 to 25
- keys: bfloat16 [2, 4608, 1536], P('cfg', 'seq'), may hold values from -25 to 25
- values: bfloat16 [2, 4608, 1536], P('cfg', 'seq'), may hold values from -6 to 6
- residual: bfloat16 [2, 4608, 3072], P('cfg', 'seq'), may hold values from -4 to 4
- gate: float32 [2, 3072], P('cfg'), may hold values from 0.5 to 4
- text_len: int32 [2], P('cfg'), may hold values from 64 to 512
- w_out: bfloat16 [1536, 3072], replicated, may hold values from -0.15625 to 0.15625
- w_final: bfloat16 [3072, 64], replicated, may hold values from -0.109375 to 0.109375
- latent: float32 [128, 2048], P('seq', 'cfg'), may hold values from -6 to 6
- owner: int32 [128], replicated, may hold values from 0 to 127, as said below
Outputs:
- hidden_out: bfloat16 [2, 4608, 3072], P('cfg', 'seq')
- latent_next: float32 [128, 2048], P('seq', 'cfg')
Inputs may be any that keep to these rules, and one draw needn't show every extreme that they name: `owner`: a permutation of the indices of seq.
All inputs are finite; a program needn't handle non-finite values.
Results may differ from a plain program's by a relative error of at most 0.0065.
Values may be sent and summed in bfloat16 or wider, within the bound.
A program may use at most 192 MiB of HBM per device.

v0:
```python
import jax
import jax.numpy as jnp
from jax import lax
from jax.sharding import PartitionSpec as P

HEADS = 12
HEAD = 128
CH = 64


def shifted(block, axis, distance):
    devices = range(lax.axis_size(axis))
    route = [((i - distance) % len(devices), i) for i in devices]
    return lax.ppermute(block, axis, route)


def partner_2(x, axis, distance):
    return lax.ppermute(x, axis, [(i, i ^ 1 << distance) for i in range(lax.axis_size(axis))])


def local(queries, keys, values, residual, gate, text_len, w_out, w_final, latent, owner):
    qloc = queries[0]
    kloc = keys[0]
    vloc = values[0]
    tokens, width = qloc.shape
    nseq = lax.axis_size("seq")
    myself = lax.axis_index("seq")
    seqlen = tokens * nseq
    textslots = seqlen // 9
    limit = text_len[0]
    scale = HEAD ** (-0.5)
    qheads = qloc.reshape(tokens, HEADS, HEAD)

    def fold(carry, kblock, vblock, start):
        count = kblock.shape[0]
        keypos = start + jnp.arange(count, dtype=jnp.int32)
        valid = (keypos >= textslots) | (keypos < limit)

        def update(state):
            top, total, accum = state
            scores = (
                jnp.einsum(
                    "qhd,khd->hqk",
                    qheads,
                    kblock.reshape(count, HEADS, HEAD),
                    preferred_element_type=jnp.float32,
                )
                * scale
            )
            scores = jnp.where(valid[None, None, :], scores, -1e30)
            newtop = jnp.maximum(top, jnp.max(scores, axis=2))
            expo = jnp.where(valid[None, None, :], jnp.exp(scores - newtop[:, :, None]), 0.0)
            factor = jnp.exp(top - newtop)
            weighted = jnp.einsum(
                "hqk,khd->hqd",
                expo.astype(jnp.bfloat16),
                vblock.reshape(count, HEADS, HEAD),
                preferred_element_type=jnp.float32,
            )
            return (
                newtop,
                total * factor + jnp.sum(expo, axis=2),
                accum * factor[:, :, None] + weighted,
            )

        empty = (start >= limit) & (start + count <= textslots)
        return lax.cond(empty, lambda state: state, update, carry)

    start_state = (
        jnp.full((HEADS, tokens), -1e30, jnp.float32),
        jnp.zeros((HEADS, tokens), jnp.float32),
        jnp.zeros((HEADS, tokens, HEAD), jnp.float32),
    )
    carry = fold(start_state, kloc, vloc, myself * tokens)

    def advance(step, state):
        kblock, vblock, inner = state
        kblock, vblock = shifted((kblock, vblock), "seq", 1)
        source = (myself - step) % nseq
        return (kblock, vblock, fold(inner, kblock, vblock, source * tokens))

    kblock, vblock, carry = lax.fori_loop(1, nseq, advance, (kloc, vloc, carry))
    top, total, accum = carry
    attn = (
        (accum / total[:, :, None]).astype(jnp.bfloat16).transpose(1, 0, 2).reshape(tokens, width)
    )
    proj = jnp.dot(attn, w_out, preferred_element_type=jnp.float32)
    stream = (residual[0].astype(jnp.float32) + gate[0][None, :] * proj).astype(jnp.bfloat16)
    is_cond = lax.axis_index("cfg") == 0
    partner = partner_2(stream, "cfg", 0)
    speed_cond = jnp.dot(
        jnp.where(is_cond, stream, partner), w_final, preferred_element_type=jnp.float32
    )
    speed_free = jnp.dot(
        jnp.where(is_cond, partner, stream), w_final, preferred_element_type=jnp.float32
    )
    guided = speed_free + 3.0 * (speed_cond - speed_free)
    gathered = lax.all_gather(guided, "seq", axis=0, tiled=True)
    columns = latent.shape[1]
    tilerows = columns * lax.axis_size("cfg") // CH
    mytile = jnp.sum(jnp.where(owner == myself, jnp.arange(nseq, dtype=jnp.int32), 0))
    picked = lax.dynamic_slice_in_dim(gathered, textslots + mytile * tilerows, tilerows, 0)
    flat = picked.reshape(tilerows * CH)
    mine = lax.dynamic_slice_in_dim(flat, lax.axis_index("cfg") * columns, columns, 0)
    latent_next = latent - 0.25 * mine.reshape(1, columns)
    return (stream[None], latent_next)


def solution(mesh):
    placed = (
        P("cfg", "seq", None),
        P("cfg", "seq", None),
        P("cfg", "seq", None),
        P("cfg", "seq", None),
        P("cfg", None),
        P("cfg"),
        P(),
        P(),
        P("seq", "cfg"),
        P(),
    )
    return jax.shard_map(
        local,
        mesh=mesh,
        in_specs=placed,
        out_specs=(P("cfg", "seq", None), P("seq", "cfg")),
        check_vma=False,
    )
```

profile of v0, /device:TPU:1, one launch (start us, length us, event | category | flops | bytes accessed | tf_op | source)
XLA Modules:
  0.0 1816.0 jit_solution(2508777275173952751)
XLA Ops:
  12.5 1645.2 %while.23 = (s32[]{:T(128)}, bf16[36,1536]{1,0:T(8,128)(2,1)S(1)}, bf16[36,1536]{1,0:T(8,128)(2,1)S(1)}, f32[12,36]{1,0:T(8,128)S(1)}, f32[12,36]{1,0:T(8,128)S(...) while((s32[]{:T(128)}, bf16[36,1536]{1,0:T(8,128)(2,1)S(1)}, ...), condition=%wide.region_9.10_spmd, body=%wide.region_4.9_spmd.sunk | while | flops 8214212 | bytes 2758840 | solution.py:82
  46.7 10.4 collective-permute-done.1
  72.9 10.4 collective-permute-done.1
  99.2 10.4 collective-permute-done.1
  125.5 10.4 collective-permute-done.1
  151.7 10.4 collective-permute-done.1
  178.0 10.4 collective-permute-done.1
  204.3 10.4 collective-permute-done.1
  230.5 10.4 collective-permute-done.1
  256.8 10.4 collective-permute-done.1
  283.0 10.4 collective-permute-done.1
  309.3 10.4 collective-permute-done.1
  335.6 10.4 collective-permute-done.1
  361.8 10.4 collective-permute-done.1
  388.1 10.4 collective-permute-done.1
  414.4 10.4 collective-permute-done.1
  440.6 10.4 collective-permute-done.1
  466.9 10.4 collective-permute-done.1
  493.2 10.4 collective-permute-done.1
  519.4 10.4 collective-permute-done.1
  545.7 10.4 collective-permute-done.1
  572.0 10.4 collective-permute-done.1
  598.2 10.4 collective-permute-done.1
  624.5 10.4 collective-permute-done.1
  650.8 10.4 collective-permute-done.1
  677.0 10.4 collective-permute-done.1
  703.3 10.4 collective-permute-done.1
  729.6 10.4 collective-permute-done.1
  755.8 10.4 collective-permute-done.1
  782.1 10.4 collective-permute-done.1
  808.4 10.4 collective-permute-done.1
  834.6 10.4 collective-permute-done.1
  860.9 10.4 collective-permute-done.1
  887.1 10.4 collective-permute-done.1
  913.4 10.4 collective-permute-done.1
  939.7 10.4 collective-permute-done.1
  965.9 10.4 collective-permute-done.1
  992.2 10.4 collective-permute-done.1
  1018.5 10.4 collective-permute-done.1
  1044.7 10.4 collective-permute-done.1
  1071.0 10.4 collective-permute-done.1
  1097.3 10.4 collective-permute-done.1
  1123.5 10.4 collective-permute-done.1
  1149.8 10.4 collective-permute-done.1
  1176.1 10.4 collective-permute-done.1
  1630.7 12.0 collective-permute-done.1
  1663.4 17.0 collective-permute-start.2
  1686.5 119.5 %all-gather.3.cloned.1.call-done = f32[128,36,64]{2,1,0:T(8,128)} async-done(((f32[1,36,64]{2,1,0:T(8,128)}), f32[128,36,64]{2,1,0:T(8,128)}) %all-gather.3.cloned.1.call-update) | async-done | bytes 1179664 | tf_op jit(solution)/shard_map/all_gather | solution.py:98
  (2086 shorter events, 1287.5 us)
Async XLA Ops:
  7.2 1798.8 %all-gather.3.cloned.1.call-start = ((), (), s32[]{:S(2)}) async-start(), calls=%async_computation | async-start | bytes 2641920 | tf_op jit(solution)/shard_map/all_gather | solution.py:98
  45.9 11.3 collective-permute-start
  72.2 11.3 collective-permute-start
  98.4 11.3 collective-permute-start
  124.7 11.3 collective-permute-start
  151.0 11.3 collective-permute-start
  177.2 11.3 collective-permute-start
  203.5 11.3 collective-permute-start
  229.8 11.3 collective-permute-start
  256.0 11.3 collective-permute-start
  282.3 11.3 collective-permute-start
  308.5 11.3 collective-permute-start
  334.8 11.3 collective-permute-start
  361.1 11.3 collective-permute-start
  387.3 11.3 collective-permute-start
  413.6 11.3 collective-permute-start
  439.9 11.3 collective-permute-start
  466.1 11.3 collective-permute-start
  492.4 11.3 collective-permute-start
  518.7 11.3 collective-permute-start
  544.9 11.3 collective-permute-start
  571.2 11.3 collective-permute-start
  597.5 11.3 collective-permute-start
  623.7 11.3 collective-permute-start
  650.0 11.3 collective-permute-start
  676.3 11.3 collective-permute-start
  702.5 11.3 collective-permute-start
  728.8 11.3 collective-permute-start
  755.1 11.3 collective-permute-start
  781.3 11.3 collective-permute-start
  807.6 11.3 collective-permute-start
  833.9 11.3 collective-permute-start
  860.1 11.3 collective-permute-start
  886.4 11.3 collective-permute-start
  912.6 11.3 collective-permute-start
  938.9 11.3 collective-permute-start
  965.2 11.3 collective-permute-start
  991.4 11.3 collective-permute-start
  1017.7 11.3 collective-permute-start
  1044.0 11.3 collective-permute-start
  1070.2 11.3 collective-permute-start
  1096.5 11.3 collective-permute-start
  1201.6 11.3 collective-permute-start
  1227.8 11.3 collective-permute-start
  1385.4 11.3 collective-permute-start
  1629.8 12.9 collective-permute-start.1
  1629.9 13.0 collective-permute-start
  1663.4 20.6 %collective-permute-start.2 = (bf16[36,3072]{1,0:T(8,128)(2,1)S(1)}, bf16[36,3072]{1,0:T(8,128)(2,1)S(1)}, u32[]{:S(2)}, u32[]{:S(2)}) collective-permute-start(bf16[36,3072]{1,0:T(8,128)(2,1)S(1)} %fusion.23), channel_id=1, source_target_pairs={{0,128},{128,0},{1,129},{129,1},{2,130},{130,2},{3,131},{131,3},{4... | collective-permute-start | bytes 663560 | tf_op jit(solution)/shard_map/ppermute | solution.py:18
  (214 other events, 7618.0 us)
Sparse Core Ops, SparseCore 0:
  1685.3 120.5 all-gather.2
where the time goes:
time: 1820 us
  waiting for transfers between devices  1450 us (80%)
  loops' own time  101 us (6%)
  other arithmetic  93.2 us (5%)
  matrix products  75.8 us (4%)
  starting transfers between devices  48.1 us (3%)
  local copies, waits for them, and re-layouts  33.9 us (2%)
    ppermute x254, waiting for transfers between devices, shifted(): return lax.ppermute(block, axis, route)  1330 us
    all_gather x1, waiting for transfers between devices, local(): gathered = lax.all_gather(guided, 'seq', axis=0, tiled=True)  119 us
    another operation x1, loops' own time, local(): kblock, vblock, carry = lax.fori_loop(1, nseq, advance, (kloc, vloc, carry))  93.6 us
    or x118, other arithmetic, fold(): valid = (keypos >= textslots) | (keypos < limit)  76.8 us
    dot_general x118, matrix products, update(): jnp.einsum('hqk,khd->hqd', expo.astype(jnp.bfloat16), vblock.reshape(coun...  43.3 us
  transfers between devices with their start and end apart: 256, of which 256 were waited for; matrix products, arithmetic and copies ran while one was open for 0% of the time, Pallas kernels for 0%

commit v1 on v0

v1 whole, which is shorter than its diff:
```python
import jax
import jax.numpy as jnp
from jax import lax
from jax.sharding import PartitionSpec as P

HEADS = 12
HEAD = 128
CH = 64


def partner_2(x, axis, distance):
    return lax.ppermute(x, axis, [(i, i ^ 1 << distance) for i in range(lax.axis_size(axis))])


def local(queries, keys, values, residual, gate, text_len, w_out, w_final, latent, owner):
    qloc = queries[0]
    kloc = keys[0]
    vloc = values[0]
    tokens, width = qloc.shape
    nseq = lax.axis_size("seq")
    myself = lax.axis_index("seq")
    seqlen = tokens * nseq
    textslots = seqlen // 9
    limit = text_len[0]
    scale = HEAD ** (-0.5)
    both = lax.all_gather(jnp.concatenate([kloc, vloc], axis=1), "seq", axis=0, tiled=True)
    qheads = qloc.reshape(tokens, HEADS, HEAD)
    kall = both[:, :width].reshape(seqlen, HEADS, HEAD)
    vall = both[:, width:].reshape(seqlen, HEADS, HEAD)
    keypos = jnp.arange(seqlen, dtype=jnp.int32)
    valid = (keypos >= textslots) | (keypos < limit)
    scores = jnp.einsum("qhd,khd->hqk", qheads, kall, preferred_element_type=jnp.float32) * scale
    scores = jnp.where(valid[None, None, :], scores, -1e30)
    top = jnp.max(scores, axis=2, keepdims=True)
    expo = jnp.where(valid[None, None, :], jnp.exp(scores - top), 0.0)
    total = jnp.sum(expo, axis=2, keepdims=True)
    accum = jnp.einsum(
        "hqk,khd->hqd", expo.astype(jnp.bfloat16), vall, preferred_element_type=jnp.float32
    )
    attn = (accum / total).astype(jnp.bfloat16).transpose(1, 0, 2).reshape(tokens, width)
    proj = jnp.dot(attn, w_out, preferred_element_type=jnp.float32)
    stream = (residual[0].astype(jnp.float32) + gate[0][None, :] * proj).astype(jnp.bfloat16)
    is_cond = lax.axis_index("cfg") == 0
    speed = jnp.dot(stream, w_final, preferred_element_type=jnp.float32)
    other = partner_2(speed, "cfg", 0)
    speed_cond = jnp.where(is_cond, speed, other)
    speed_free = jnp.where(is_cond, other, speed)
    guided = speed_free + 3.0 * (speed_cond - speed_free)
    gathered = lax.all_gather(guided, "seq", axis=0, tiled=True)
    columns = latent.shape[1]
    tilerows = columns * lax.axis_size("cfg") // CH
    mytile = jnp.sum(jnp.where(owner == myself, jnp.arange(nseq, dtype=jnp.int32), 0))
    picked = lax.dynamic_slice_in_dim(gathered, textslots + mytile * tilerows, tilerows, 0)
    flat = picked.reshape(tilerows * CH)
    mine = lax.dynamic_slice_in_dim(flat, lax.axis_index("cfg") * columns, columns, 0)
    latent_next = latent - 0.25 * mine.reshape(1, columns)
    return (stream[None], latent_next)


def solution(mesh):
    placed = (
        P("cfg", "seq", None),
        P("cfg", "seq", None),
        P("cfg", "seq", None),
        P("cfg", "seq", None),
        P("cfg", None),
        P("cfg"),
        P(),
        P(),
        P("seq", "cfg"),
        P(),
    )
    return jax.shard_map(
        local,
        mesh=mesh,
        in_specs=placed,
        out_specs=(P("cfg", "seq", None), P("seq", "cfg")),
        check_vma=False,
    )
```

time: 1820 us -> 470 us (0.26)
  waiting for transfers between devices: 1450 us -> 326 us
  loops' own time: 101 us -> 0 us
  other arithmetic: 93.2 us -> 8.35 us
  local copies, waits for them, and re-layouts: 33.9 us -> 95 us
  matrix products: 75.8 us -> 22.9 us
  starting transfers between devices: 48.1 us -> 0.41 us
    ppermute x254 -> x0, waiting for transfers between devices: 1330 us -> none  [shifted(): return lax.ppermute(block, axis, route)]
    all_gather x0 -> x1, waiting for transfers between devices: none -> 210 us  [local(): lax.all_gather(jnp.concatenate([kloc, vloc], axis=1), 'seq', axis=0, tile...]
    another operation x129 -> x0, loops' own time: 101 us -> none  [the longest x1 93.6 us: local(): kblock, vblock, carry = lax.fori_loop(1, nseq, advance, (kloc, vloc, carry))]
    or x118 -> x1, other arithmetic: 76.8 us -> 0.01 us  [local(): valid = (keypos >= textslots) | (keypos < limit)]
    slice x0 -> x3, local copies, waits for them, and re-layouts: none -> 58 us  [the longest x2 39.4 us: local(): kall = both[:, :width].reshape(seqlen, HEADS, HEAD)]
    dot_general x238 -> x3, matrix products: 70.4 us -> 17.5 us  [the longest x1 11.1 us: local(): jnp.einsum('hqk,khd->hqd', expo.astype(jnp.bfloat16), vall, preferred_ele...]
    unnamed x17 -> x16, local copies, waits for them, and re-layouts: 4.39 us -> 35.9 us
    ppermute x254 -> x0, starting transfers between devices: 31 us -> none  [shifted(): return lax.ppermute(block, axis, route)]
  transfers between devices with their start and end apart: 256 -> 3, of which waited for: 256 -> 3; matrix products, arithmetic and copies ran while one was open for 0% -> 0% of each run, Pallas kernels for 0% -> 0%
where the time goes in v1:
time: 470 us; the launch traced here: 468 us
  waiting for transfers between devices  326 us (69%)
  local copies, waits for them, and re-layouts  95 us (20%)
  matrix products  22.9 us (5%)
  between operations  15.5 us (3%)
  other arithmetic  8.35 us (2%)
    all_gather x1, waiting for transfers between devices, local(): lax.all_gather(jnp.concatenate([kloc, vloc], axis=1), 'seq', axis=0, tile...  210 us
    all_gather x1, waiting for transfers between devices, local(): gathered = lax.all_gather(guided, 'seq', axis=0, tiled=True)  114 us
    slice x2, local copies, waits for them, and re-layouts, local(): kall = both[:, :width].reshape(seqlen, HEADS, HEAD)  39.4 us
    unnamed x16, local copies, waits for them, and re-layouts  35.9 us
    slice x1, local copies, waits for them, and re-layouts, local(): vall = both[:, width:].reshape(seqlen, HEADS, HEAD)  18.5 us
    dot_general x1, matrix products, local(): jnp.einsum('hqk,khd->hqd', expo.astype(jnp.bfloat16), vall, preferred_ele...  11.1 us
  transfers between devices with their start and end apart: 3, of which 3 were waited for; matrix products, arithmetic and copies ran while one was open for 0% of the time, Pallas kernels for 0%

profile of v1, /device:TPU:1, one launch (start us, length us, event | category | flops | bytes accessed | tf_op | source)
XLA Modules:
  0.0 468.3 jit_solution(7332716834692380684)
XLA Ops:
  7.2 0.0 copy-start
  7.2 0.0 all-gather.5.cloned.1.call-start
  7.2 1.7 maximum_bitcast_fusion
  8.9 0.0 all-gather.5.cloned.1.call-update
  9.0 0.0 all-gather.7.cloned.1.call-start
  9.7 1.0 reshape_squeeze.3
  10.7 210.0 %all-gather.5.cloned.1.call-done = bf16[128,36,3072]{2,1,0:T(8,128)(2,1)} async-done(((bf16[1,36,3072]{2,1,0:T(8,128)(2,1)}), bf16[128,36,3072]{2,1,0:T(8,128)(2,1)}) %all-gather.5.cloned.1.call-update) | async-done | bytes 28311568 | tf_op jit(solution)/shard_map/all_gather | solution.py:26
  220.7 33.4 %reshape.35 = bf16[4608,3072]{1,0:T(8,128)(2,1)} reshape(bf16[128,36,3072]{2,1,0:T(8,128)(2,1)} %all-gather.5.cloned.1.call-done) | data formatting | bytes 56623104
  254.1 20.7 %fusion.21 = (bf16[4608,1536]{1,0:T(8,128)(2,1)}, bf16[4608,1536]{1,0:T(8,128)(2,1)}) fusion(bf16[4608,3072]{1,0:T(8,128)(2,1)} %reshape.35), kind=kLoop, calls=%fused_computation.24 | loop fusion | bytes 56623104 | tf_op jit(solution)/shard_map/slice | solution.py:28
  274.7 18.8 %copy.19 = bf16[4608,1536]{0,1:T(8,128)(2,1)} copy(bf16[4608,1536]{1,0:T(8,128)(2,1)} %get-tuple-element.2) | data formatting | bytes 28311552 | tf_op jit(solution)/shard_map/slice | solution.py:28
  293.5 6.2 %multiply_select_fusion = f32[12,4608,36]{1,2,0:T(8,128)S(1)} fusion(bf16[4608,12,128]{0,2,1:T(8,128)(2,1)} %bitcast.41, pred[4608]{0:T(1024)(128)(4,1)S(1)} %fusion.19, bf16[36,12,128]{2,1,0:T(8,128)(2,1)S(1)} %reshape_squeeze.3), kind=kOutput, calls=%fused_computation.5 | convolution fusion | flops 513589248 | bytes 22233600 | tf_op jit(solution)/shard_map/qhd,khd->hqk/dot_general | solution.py:32
  299.7 4.8 %fusion.22 = (f32[12,36]{1,0:T(8,128)S(1)}, bf16[12,36,4608]{2,1,0:T(8,128)(2,1)}) fusion(f32[12,4608,36]{1,2,0:T(8,128)S(1)} %multiply_select_fusion, pred[4608]{0:T(1024)(128)(4,1)S(1)} %fusion.19), kind=kOutput, calls=%fused_computation.25 | output fusion | flops 7967231 | bytes 11950272 | tf_op jit(solution)/shard_map/sub | solution.py:35
  304.5 18.5 %copy.22 = bf16[4608,1536]{0,1:T(8,128)(2,1)} copy(bf16[4608,1536]{1,0:T(8,128)(2,1)} %get-tuple-element.3) | data formatting | bytes 28311552 | tf_op jit(solution)/shard_map/slice | solution.py:29
  323.0 0.0 copy-start.2
  323.0 0.0 copy-start.3
  323.0 11.1 %fusion.15 = bf16[36,12,128]{2,0,1:T(8,128)(2,1)S(1)} fusion(bf16[4608,12,128]{0,2,1:T(8,128)(2,1)} %bitcast.42, bf16[12,36,4608]{2,1,0:T(8,128)(2,1)} %get-tuple-element.5, f32[36,12]{0,1:T(8,128)S(1)} %bitcast.50), kind=kOutput, calls=%fused_computation.13 | convolution fusion | flops 509718528 | bytes 18249408 | tf_op jit(solution)/shard_map/hqk,khd->hqd/dot_general | solution.py:37
  334.2 0.0 copy-start.5
  334.3 0.0 copy-done.2
  334.3 0.0 copy-done.3
  334.3 0.0 copy-start.4
  334.3 5.4 %fusion.8 = bf16[36,3072]{1,0:T(8,128)(2,1)S(1)} fusion(bf16[36,1536]{1,0:T(8,128)(2,1)S(1)} %bitcast.44, bf16[1536,3072]{1,0:T(8,128)(2,1)} %param.16, bf16[1,36,3072]{2,1,0:T(8,128)(2,1)S(1)} %copy-done.2, f32[3072]{0:T(1024)S(1)} %bitcast.49), kind=kOutput, calls=%fused_computation.10 | convolution fusion | flops 340180992 | bytes 10002432 | tf_op jit(solution)/shard_map/dot_general | solution.py:41
  339.7 0.0 copy-done
  339.7 0.0 copy-start.1
  339.7 0.2 fusion.23
  340.0 0.3 collective-permute-start
  340.3 2.4 collective-permute-done
  342.7 0.6 add_bitcast_fusion
  343.3 0.0 all-gather.7.cloned.1.call-update
  343.3 0.0 copy-done.5
  343.3 0.6 fusion.20
  344.6 113.7 %all-gather.7.cloned.1.call-done = f32[128,36,64]{2,1,0:T(8,128)} async-done(((f32[1,36,64]{2,1,0:T(8,128)}), f32[128,36,64]{2,1,0:T(8,128)}) %all-gather.7.cloned.1.call-update) | async-done | bytes 1179664 | tf_op jit(solution)/shard_map/all_gather | solution.py:49
  458.3 2.4 reshape.37
  460.7 0.1 reshape.32
  460.8 0.0 copy-done.4
  460.8 0.6 sub.17
  461.4 0.0 copy-done.1
  (6 shorter events, 0.1 us)
Async XLA Ops:
  7.2 332.6 %copy-start = (bf16[3072,64]{0,1:T(8,128)(2,1)S(1)}, bf16[3072,64]{0,1:T(8,128)(2,1)}, u32[]{:S(2)}) copy-start(bf16[3072,64]{0,1:T(8,128)(2,1)} %param.17) | copy-start | bytes 1179652
  7.2 213.5 %all-gather.5.cloned.1.call-start = ((), (), s32[]{:S(2)}) async-start(), calls=%async_computation | async-start | bytes 31703040 | tf_op jit(solution)/shard_map/all_gather | solution.py:26
  9.0 449.3 %all-gather.7.cloned.1.call-start = ((), (), s32[]{:S(2)}) async-start(), calls=%async_computation.1 | async-start | bytes 2641920 | tf_op jit(solution)/shard_map/all_gather | solution.py:49
  323.0 11.2 %copy-start.2 = (bf16[1,36,3072]{2,1,0:T(8,128)(2,1)S(1)}, bf16[1,36,3072]{2,1,0:T(8,128)(2,1)}, u32[]{:S(2)}) copy-start(bf16[1,36,3072]{2,1,0:T(8,128)(2,1)} %param.13) | copy-start | bytes 663556
  323.0 11.2 %copy-start.3 = (f32[1,3072]{1,0:T(1,128)S(1)}, f32[1,3072]{1,0:T(1,128)}, u32[]{:S(2)}) copy-start(f32[1,3072]{1,0:T(1,128)} %param.14) | copy-start | bytes 36868
  334.2 9.1 %copy-start.5 = (s32[128]{0:T(128)S(1)}, s32[128]{0:T(128)}, u32[]{:S(2)}) copy-start(s32[128]{0:T(128)} %param.19) | copy-start | bytes 1540
  334.3 126.5 %copy-start.4 = (f32[1,1024]{1,0:T(1,128)S(1)}, f32[1,1024]{1,0:T(1,128)}, u32[]{:S(2)}) copy-start(f32[1,1024]{1,0:T(1,128)} %param.18) | copy-start | bytes 12292
  339.7 121.7 %copy-start.1 = (bf16[36,3072]{1,0:T(8,128)(2,1)}, bf16[36,3072]{1,0:T(8,128)(2,1)S(1)}, u32[]{:S(2)}) copy-start(bf16[36,3072]{1,0:T(8,128)(2,1)S(1)} %fusion.8) | copy-start | bytes 663556
  340.0 2.7 collective-permute-start
Sparse Core Ops, SparseCore 0:
  12.4 208.1 all-gather.4
  343.4 114.8 all-gather.6

commit v2 on v1

v2 whole, which is shorter than its diff:
```python
import functools
import math

import jax
import jax.numpy as jnp
from jax import lax
from jax.experimental import pallas as pl
from jax.experimental.pallas import tpu as pltpu
from jax.sharding import PartitionSpec as P

HEADS = 12
HEAD = 128
CH = 64
RING = 4
PLANES = 8
GROUPS = 4
MINE = HEADS // GROUPS
MESH = pl.DeviceIdType.MESH
NEG = -1e30

ORDER = [(0, 0), (3, 0), (1, 0), (0, 3), (0, 1), (2, 0), (3, 3), (3, 1)]
ORDER += [(1, 3), (1, 1), (0, 2), (2, 3), (2, 1), (3, 2), (1, 2), (2, 2)]
READY = {ab: max(ORDER.index(ab), ORDER.index(ab[::-1])) for ab in ORDER}
SLOT = {ab: p for p, ab in enumerate(sorted(ORDER, key=lambda ab: (READY[ab], ORDER.index(ab))))}
BLOCKS = sorted(ORDER, key=lambda ab: SLOT[ab])
PER = 4


def attention_kernel(
    text_slots,
    limit_ref,
    q_ref,
    k_ref,
    v_ref,
    residual_ref,
    gate_ref,
    w_out_ref,
    w_final_ref,
    hidden_ref,
    guided_ref,
    w_out,
    limit_own,
    limit_in,
    q_in,
    k_in,
    v_in,
    wide,
    q_all,
    k_all,
    v_all,
    top,
    total,
    accum,
    o_out,
    attn,
    speed,
    speed_in,
    w_sem,
    send_sem,
    in_sem,
    self_sem,
    k_sem,
    v_sem,
    k_pair_sem,
    v_pair_sem,
    o_sem,
    speed_sem,
):
    rows = q_ref.shape[0]
    cols = MINE * HEAD
    keys = RING * rows
    cut = (keys // 2 + 15) // 16 * 16
    cfg = lax.axis_index("cfg")
    seq = lax.axis_index("seq")
    core = lax.rem(seq, 2)
    xh = lax.rem(seq // 2, 2)
    z = lax.rem(seq // 4, PLANES)
    y = seq // (4 * PLANES)
    x = 2 * xh + cfg
    half = lax.rem(z, 2)
    group = z // 2

    def device(x_at, y_at, z_at, core_at):
        return (lax.rem(x_at, 2), ((y_at * PLANES + z_at) * 2 + x_at // 2) * 2 + core_at)

    def peer(j):
        return device(2 * xh + half, y, 2 * j + cfg, core)

    def beside(axis, step):
        if axis == 0:
            return device(lax.rem(x + step + RING, RING), y, z, core)
        return device(x, lax.rem(y + step + RING, RING), z, core)

    partner = device(x, y, z, 1 - core)
    at_home = cfg == half

    w_copy = pltpu.make_async_copy(w_out_ref, w_out, w_sem)
    w_copy.start()
    limit_own[...] = jnp.full(limit_own.shape, limit_ref[0], jnp.int32)

    barrier = pltpu.get_barrier_semaphore()
    for j in range(GROUPS):
        mine = at_home & (group == j)

        @pl.when(jnp.logical_not(mine))
        def _():
            pl.semaphore_signal(barrier, inc=1, device_id=peer(j), device_id_type=MESH)

    for other in (beside(0, 1), beside(0, -1), beside(1, 1), beside(1, -1), partner):
        pl.semaphore_signal(barrier, inc=1, device_id=other, device_id_type=MESH)
    pl.semaphore_wait(barrier, jnp.where(at_home, GROUPS + 4, GROUPS + 5))

    sent = []

    def send(src, dst, arrival, where):
        copy = pltpu.make_async_remote_copy(
            src_ref=src,
            dst_ref=dst,
            send_sem=send_sem.at[len(sent)],
            recv_sem=arrival,
            device_id=where,
            device_id_type=MESH,
        )
        copy.start()
        sent.append(copy)

    spread = []

    def scatter(src, dst, arrival, j, at):
        mine = at_home & (group == j)
        remote = pltpu.make_async_remote_copy(
            src_ref=src,
            dst_ref=dst,
            send_sem=self_sem.at[at],
            recv_sem=arrival,
            device_id=peer(j),
            device_id_type=MESH,
        )
        local = pltpu.make_async_copy(src, dst, arrival)

        @pl.when(mine)
        def _():
            local.start()

        @pl.when(jnp.logical_not(mine))
        def _():
            remote.start()

        spread.append((mine, remote))

    def arrived(ref, sem):
        pltpu.make_async_copy(ref, ref, sem).wait()

    packs = ((k_ref, k_in), (v_ref, v_in), (q_ref, q_in))
    for t, (src, dst) in enumerate(packs):
        for g in range(GROUPS):
            scatter(
                src.at[:, pl.ds(g * cols, cols)],
                dst.at[group],
                in_sem.at[t, group],
                g,
                t * GROUPS + g,
            )
    for g in range(GROUPS):
        scatter(limit_own, limit_in.at[group], in_sem.at[3, group], g, 3 * GROUPS + g)

    def compact(t, landed):
        for j in range(RING):
            arrived(landed.at[j], in_sem.at[t, j])
            wide[pl.ds(j * rows, rows), :] = landed[j].astype(jnp.float32)
        return wide[...].astype(jnp.bfloat16)

    def place(ab, values):
        return SLOT[ab[::-1]] if values else SLOT[ab]

    def have(ab, values):
        a, b = ab
        store, arrive, pair = (v_all, v_sem, v_pair_sem) if values else (k_all, k_sem, k_pair_sem)
        first, second = (1, 0) if values else (0, 1)
        p = place(ab, values)

        def whole(axis, step, to):
            s = place(to, values)
            send(store.at[2 * p], store.at[2 * s], arrive.at[s, 0], beside(axis, step))

        def part(axis, step, to, which):
            s = place(to, values)
            span = pl.ds(0, cut) if which == 0 else pl.ds(cut, keys - cut)
            send(
                store.at[2 * p, span],
                store.at[2 * s, span],
                arrive.at[s, which],
                beside(axis, step),
            )

        if b == 0:
            if a == 0:
                whole(first, 1, (3, 0))
                whole(first, -1, (1, 0))
            if a == 3:
                part(first, 1, (2, 0), 0)
            if a == 1:
                part(first, -1, (2, 0), 1)
            whole(second, 1, (a, 3))
            whole(second, -1, (a, 1))
        if b == 3:
            part(second, 1, (a, 2), 0)
        if b == 1:
            part(second, -1, (a, 2), 1)
        send(store.at[2 * p], store.at[2 * p + 1], pair.at[p], partner)

    def await_block(ab, values):
        a, b = ab
        store, arrive = (v_all, v_sem) if values else (k_all, k_sem)
        p = place(ab, values)
        if b == 2 or (b == 0 and a == 2):
            arrived(store.at[2 * p, pl.ds(0, cut)], arrive.at[p, 0])
            arrived(store.at[2 * p, pl.ds(cut, keys - cut)], arrive.at[p, 1])
        else:
            arrived(store.at[2 * p], arrive.at[p, 0])

    k_all[2 * SLOT[(0, 0)]] = compact(0, k_in)
    have((0, 0), False)
    v_all[2 * SLOT[(0, 0)]] = compact(1, v_in)
    have((0, 0), True)
    q_all[...] = compact(2, q_in)
    for j in range(RING):
        arrived(limit_in.at[j], in_sem.at[3, j])

    top[...] = jnp.full(top.shape, NEG, jnp.float32)
    total[...] = jnp.zeros(total.shape, jnp.float32)
    accum[...] = jnp.zeros(accum.shape, jnp.float32)
    factor = HEAD**-0.5 * math.log2(math.e)

    def bias_of(ab, other):
        x_at = lax.rem(x + ab[0], RING)
        y_at = lax.rem(y + ab[1], RING)
        core_at = 1 - core if other else core
        n = lax.broadcasted_iota(jnp.int32, (1, keys), 1)
        j = sum((n >= rows * i).astype(jnp.int32) for i in range(1, RING))
        holder = ((y_at * PLANES + 2 * j + lax.rem(x_at, 2)) * 2 + x_at // 2) * 2 + core_at
        pos = holder * rows + n - rows * j
        limit = limit_in[0, 0:1, :]
        limit = jnp.concatenate([limit, limit[:, : keys - 128]], axis=1)
        return jnp.where((pos >= text_slots) | (pos < limit), 0.0, NEG)

    def fold(at):
        for ab in BLOCKS[at * PER : (at + 1) * PER]:
            p = SLOT[ab]
            if ab != (0, 0) or True:
                arrived(k_all.at[2 * p + 1], k_pair_sem.at[p])
                arrived(v_all.at[2 * p + 1], v_pair_sem.at[p])
        bias = jnp.concatenate(
            [bias_of(ab, o) for ab in BLOCKS[at * PER : (at + 1) * PER] for o in range(2)], axis=1
        )
        span = pl.ds(at * PER * 2, PER * 2)
        many = PER * 2 * keys
        for h in range(MINE):
            lanes = slice(h * HEAD, (h + 1) * HEAD)
            kk = k_all[span, :, lanes].reshape(many, HEAD)
            vv = v_all[span, :, lanes].reshape(many, HEAD)
            scores = lax.dot_general(
                q_all[:, lanes], kk, (((1,), (1,)), ((), ())), preferred_element_type=jnp.float32
            )
            scores = scores * factor + bias
            old = top[h]
            new = jnp.maximum(old, jnp.max(scores, axis=1, keepdims=True))
            expo = jnp.exp2(scores - new[:, :1])
            shrink = jnp.exp2(old - new)
            top[h] = new
            total[h] = total[h] * shrink + jnp.sum(expo, axis=1, keepdims=True)
            accum[h] = accum[h] * shrink + jnp.dot(
                expo.astype(jnp.bfloat16), vv, preferred_element_type=jnp.float32
            )

    done = 0
    for n, ab in enumerate(ORDER):
        if n == 0:
            continue
        await_block(ab, False)
        have(ab, False)
        await_block(ab, True)
        have(ab, True)
        while (done + 1) * PER < len(BLOCKS) and READY[BLOCKS[(done + 1) * PER - 1]] < n:
            fold(done)
            done += 1
    while done * PER < len(BLOCKS):
        fold(done)
        done += 1

    for h in range(MINE):
        wide[:, pl.ds(h * HEAD, HEAD)] = accum[h] / total[h]
    for j in range(RING):
        o_out[j] = wide[pl.ds(j * rows, rows), :].astype(jnp.bfloat16)
    at_cols = pl.ds(pl.multiple_of(group * cols, cols), cols)
    for j in range(RING):
        scatter(o_out.at[j], attn.at[:, at_cols], o_sem.at[group], j, 4 * GROUPS + j)
    w_copy.wait()
    for g in range(GROUPS):
        arrived(attn.at[:, pl.ds(g * cols, cols)], o_sem.at[g])

    width = hidden_ref.shape[1]
    step = 512
    rate = jnp.zeros(speed.shape, jnp.float32)
    for at in range(0, width, step):
        lanes = slice(at, at + step)
        proj = jnp.dot(attn[...], w_out[:, lanes], preferred_element_type=jnp.float32)
        stream = residual_ref[:, lanes].astype(jnp.float32) + gate_ref[:, lanes] * proj
        stream = stream.astype(jnp.bfloat16)
        hidden_ref[:, lanes] = stream
        rate += jnp.dot(stream, w_final_ref[lanes, :], preferred_element_type=jnp.float32)
    speed[...] = rate
    to = beside_cfg = device(2 * xh + 1 - cfg, y, z, core)
    send(speed, speed_in, speed_sem, to)
    arrived(speed_in, speed_sem)
    other = speed_in[...]
    cond = jnp.where(cfg == 0, rate, other)
    free = jnp.where(cfg == 0, other, rate)
    guided_ref[...] = free + 3.0 * (cond - free)

    for copy in sent:
        copy.wait_send()
    for mine, copy in spread:

        @pl.when(jnp.logical_not(mine))
        def _():
            copy.wait_send()


def local(queries, keys, values, residual, gate, text_len, w_out, w_final, latent, owner):
    tokens, width = queries.shape[1:]
    nseq = lax.axis_size("seq")
    myself = lax.axis_index("seq")
    seqlen = tokens * nseq
    textslots = seqlen // 9
    cols = MINE * HEAD
    block = RING * tokens
    vmem = pl.BlockSpec(memory_space=pltpu.VMEM)
    bf16, f32 = jnp.bfloat16, jnp.float32
    dma = pltpu.SemaphoreType.DMA
    stream, guided = pl.pallas_call(
        functools.partial(attention_kernel, textslots),
        out_shape=(
            jax.ShapeDtypeStruct(residual.shape[1:], bf16),
            jax.ShapeDtypeStruct((tokens, CH), f32),
        ),
        in_specs=[pl.BlockSpec(memory_space=pltpu.SMEM)]
        + [vmem] * 5
        + [pl.BlockSpec(memory_space=pl.ANY), vmem],
        out_specs=(vmem, vmem),
        scratch_shapes=[
            pltpu.VMEM(w_out.shape, bf16),
            pltpu.VMEM((8, 128), jnp.int32),
            pltpu.VMEM((RING, 8, 128), jnp.int32),
            pltpu.VMEM((RING, tokens, cols), bf16),
            pltpu.VMEM((RING, tokens, cols), bf16),
            pltpu.VMEM((RING, tokens, cols), bf16),
            pltpu.VMEM((block, cols), f32),
            pltpu.VMEM((block, cols), bf16),
            pltpu.VMEM((2 * len(ORDER), block, cols), bf16),
            pltpu.VMEM((2 * len(ORDER), block, cols), bf16),
            pltpu.VMEM((MINE, block, HEAD), f32),
            pltpu.VMEM((MINE, block, HEAD), f32),
            pltpu.VMEM((MINE, block, HEAD), f32),
            pltpu.VMEM((RING, tokens, cols), bf16),
            pltpu.VMEM((tokens, width), bf16),
            pltpu.VMEM((tokens, CH), f32),
            pltpu.VMEM((tokens, CH), f32),
            dma,
            dma((73,)),
            dma((4, RING)),
            dma((20,)),
            dma((len(ORDER), 2)),
            dma((len(ORDER), 2)),
            dma((len(ORDER),)),
            dma((len(ORDER),)),
            dma((GROUPS,)),
            dma,
        ],
        compiler_params=pltpu.CompilerParams(
            collective_id=0, has_side_effects=True, vmem_limit_bytes=60 * 1024 * 1024
        ),
    )(text_len, queries[0], keys[0], values[0], residual[0], gate, w_out, w_final)
    gathered = lax.all_gather(guided, "seq", axis=0, tiled=True)
    columns = latent.shape[1]
    tilerows = columns * lax.axis_size("cfg") // CH
    mytile = jnp.sum(jnp.where(owner == myself, jnp.arange(nseq, dtype=jnp.int32), 0))
    picked = lax.dynamic_slice_in_dim(gathered, textslots + mytile * tilerows, tilerows, 0)
    flat = picked.reshape(tilerows * CH)
    mine = lax.dynamic_slice_in_dim(flat, lax.axis_index("cfg") * columns, columns, 0)
    latent_next = latent - 0.25 * mine.reshape(1, columns)
    return (stream[None], latent_next)


def solution(mesh):
    placed = (
        P("cfg", "seq", None),
        P("cfg", "seq", None),
        P("cfg", "seq", None),
        P("cfg", "seq", None),
        P("cfg", None),
        P("cfg"),
        P(),
        P(),
        P("seq", "cfg"),
        P(),
    )
    return jax.shard_map(
        local,
        mesh=mesh,
        in_specs=placed,
        out_specs=(P("cfg", "seq", None), P("seq", "cfg")),
        check_vma=False,
    )
```

time: 470 us -> 197 us (0.42)
  waiting for transfers between devices: 326 us -> 116 us
  local copies, waits for them, and re-layouts: 95 us -> 5.39 us
  Pallas kernels: 0 us -> 58.9 us
  matrix products: 22.9 us -> 0 us
  other arithmetic: 8.35 us -> 1.24 us
    all_gather x1 -> x0, waiting for transfers between devices: 210 us -> none  [local(): lax.all_gather(jnp.concatenate([kloc, vloc], axis=1), 'seq', axis=0, tile...]
    pallas_call x0 -> x1, Pallas kernels: none -> 58.9 us  [local(): pl.pallas_call(functools.partial(attention_kernel, textslots), out_shape=...]
    slice x3 -> x0, local copies, waits for them, and re-layouts: 58 us -> none  [the longest x2 39.4 us: local(): kall = both[:, :width].reshape(seqlen, HEADS, HEAD)]
    unnamed x16 -> x9, local copies, waits for them, and re-layouts: 35.9 us -> 5.31 us
    dot_general x4 -> x0, matrix products: 22.9 us -> none  [the longest x1 11.1 us: local(): jnp.einsum('hqk,khd->hqd', expo.astype(jnp.bfloat16), vall, preferred_ele...]
    sub x1 -> x0, other arithmetic: 4.79 us -> none  [local(): expo = jnp.where(valid[None, None, :], jnp.exp(scores - top), 0.0)]
  transfers between devices with their start and end apart: 3 -> 1, of which waited for: 3 -> 1; matrix products, arithmetic and copies ran while one was open for 0% -> 0% of each run, Pallas kernels for 0% -> 0%
where the time goes in v2:
time: 197 us
  waiting for transfers between devices  116 us (59%)
  Pallas kernels  58.9 us (30%)
  between operations  15.4 us (8%)
  local copies, waits for them, and re-layouts  5.39 us (3%)
    all_gather x1, waiting for transfers between devices, local(): gathered = lax.all_gather(guided, 'seq', axis=0, tiled=True)  116 us
    pallas_call x1, Pallas kernels, local(): pl.pallas_call(functools.partial(attention_kernel, textslots), out_shape=...  58.9 us
    unnamed x9, local copies, waits for them, and re-layouts  5.31 us
  transfers between devices with their start and end apart: 1, of which 1 were waited for; matrix products, arithmetic and copies ran while one was open for 0% of the time, Pallas kernels for 0%

profile of v2, /device:TPU:1, one launch (start us, length us, event | category | flops | bytes accessed | tf_op | source)
XLA Modules:
  0.0 197.2 jit_solution(8348958653694854041)
XLA Ops:
  7.2 0.0 all-gather.3.cloned.1.call-start
  7.9 2.2 %copy.14.w_final_ref = bf16[3072,64]{1,0:T(8,128)(2,1)} copy(bf16[3072,64]{0,1:T(8,128)(2,1)} %param.17) | data formatting | bytes 786432 | tf_op args[7]
  10.0 0.0 copy-start.2
  10.0 58.9 %shard_map.113 = (bf16[36,3072]{1,0:T(8,128)(2,1)}, f32[36,64]{1,0:T(8,128)}) custom-call(s32[1]{0:T(128)S(6)} %copy.16.limit_ref, bf16[36,1536]{1,0:T(8,128)(2,1)} %bitcast.9, bf16[36,1536]{1,0:T(8,128)(2,1)} %bitcast.10, bf16[36,1536]{1,0:T(8,128)(2,1)} %bitcast.11, bf16[36,3072]{1,0:T(8,128)(2,1)} %bitcast.7, f32[1,3072]{1,0:T(1,128)} %gate_ref.1, ...), custom_call_target="tpu_custom_call" | custom-call | tf_op jit(solution)/shard_map/pallas_call | solution.py:341
  68.9 0.0 copy-start.1
  68.9 0.0 copy-start
  68.9 0.0 all-gather.3.cloned.1.call-update
  69.0 0.0 copy-done.2
  69.0 0.6 fusion
  70.3 116.2 %all-gather.3.cloned.1.call-done = f32[128,36,64]{2,1,0:T(8,128)} async-done(((f32[1,36,64]{2,1,0:T(8,128)}), f32[128,36,64]{2,1,0:T(8,128)}) %all-gather.3.cloned.1.call-update) | async-done | bytes 1179664 | tf_op jit(solution)/shard_map/all_gather | solution.py:384
  186.5 2.4 %reshape.11 = f32[4608,64]{1,0:T(8,128)S(1)} reshape(f32[128,36,64]{2,1,0:T(8,128)} %all-gather.3.cloned.1.call-done) | data formatting | bytes 2359296
  189.0 0.1 reshape.9
  189.1 0.0 copy-done.1
  189.1 0.6 sub.3
  189.7 0.0 copy-done
  189.7 0.7 copy.17
  (2 shorter events, 0.0 us)
Async XLA Ops:
  7.2 179.4 %all-gather.3.cloned.1.call-start = ((), (), s32[]{:S(2)}) async-start(), calls=%async_computation | async-start | bytes 2641920 | tf_op jit(solution)/shard_map/all_gather | solution.py:384
  10.0 59.0 %copy-start.2 = (s32[128]{0:T(128)S(1)}, s32[128]{0:T(128)}, u32[]{:S(2)}) copy-start(s32[128]{0:T(128)} %param.19) | copy-start | bytes 1540
  68.9 120.1 %copy-start.1 = (f32[1,1024]{1,0:T(1,128)S(1)}, f32[1,1024]{1,0:T(1,128)}, u32[]{:S(2)}) copy-start(f32[1,1024]{1,0:T(1,128)} %param.18) | copy-start | bytes 12292
  68.9 120.7 %copy-start = (bf16[36,3072]{1,0:T(8,128)(2,1)S(1)}, bf16[36,3072]{1,0:T(8,128)(2,1)}, u32[]{:S(2)}) copy-start(bf16[36,3072]{1,0:T(8,128)(2,1)} %get-tuple-element.4) | copy-start | bytes 663556
Sparse Core Ops, SparseCore 0:
  69.1 117.3 all-gather.2

commit v3 on v2

--- a/solution.py
+++ b/solution.py
@@ -24,11 +24,13 @@
 SLOT = {ab: p for p, ab in enumerate(sorted(ORDER, key=lambda ab: (READY[ab], ORDER.index(ab))))}
 BLOCKS = sorted(ORDER, key=lambda ab: SLOT[ab])
 PER = 4
+PART = 16
 
 
 def attention_kernel(
     text_slots,
     limit_ref,
+    tile_ref,
     q_ref,
     k_ref,
     v_ref,
@@ -37,7 +39,7 @@
     w_out_ref,
     w_final_ref,
     hidden_ref,
-    guided_ref,
+    mine_ref,
     w_out,
     limit_own,
     limit_in,
@@ -55,6 +57,8 @@
     attn,
     speed,
     speed_in,
+    aligned,
+    tiles,
     w_sem,
     send_sem,
     in_sem,
@@ -65,6 +69,10 @@
     v_pair_sem,
     o_sem,
     speed_sem,
+    x_sem,
+    z_sem,
+    y_sem,
+    core_sem,
 ):
     rows = q_ref.shape[0]
     cols = MINE * HEAD
@@ -106,9 +114,13 @@
         def _():
             pl.semaphore_signal(barrier, inc=1, device_id=peer(j), device_id_type=MESH)
 
-    for other in (beside(0, 1), beside(0, -1), beside(1, 1), beside(1, -1), partner):
+    across = device(lax.rem(x + 2, RING), y, z, core)
+    planes = [device(x, y, lax.rem(z + d, PLANES), core) for d in range(1, PLANES)]
+    others = [beside(0, 1), beside(0, -1), beside(1, 1), beside(1, -1), partner]
+    others += [across, beside(1, 2)] + planes
+    for other in others:
         pl.semaphore_signal(barrier, inc=1, device_id=other, device_id_type=MESH)
-    pl.semaphore_wait(barrier, jnp.where(at_home, GROUPS + 4, GROUPS + 5))
+    pl.semaphore_wait(barrier, GROUPS + len(others) - at_home.astype(jnp.int32))
 
     sent = []
 
@@ -310,13 +322,57 @@
         hidden_ref[:, lanes] = stream
         rate += jnp.dot(stream, w_final_ref[lanes, :], preferred_element_type=jnp.float32)
     speed[...] = rate
-    to = beside_cfg = device(2 * xh + 1 - cfg, y, z, core)
+    to = device(2 * xh + 1 - cfg, y, z, core)
     send(speed, speed_in, speed_sem, to)
     arrived(speed_in, speed_sem)
     other = speed_in[...]
     cond = jnp.where(cfg == 0, rate, other)
     free = jnp.where(cfg == 0, other, rate)
-    guided_ref[...] = free + 3.0 * (cond - free)
+    aligned[...] = jnp.zeros(aligned.shape, jnp.float32)
+    aligned[pl.ds(0, rows), pl.ds(0, CH)] = free + 3.0 * (cond - free)
+    rolled = pltpu.roll(aligned[...], lax.rem(rows * seq, 2 * PART), 0)
+    parts = [rolled[i * PART : (i + 1) * PART] for i in range(4)]
+    near = jnp.where(cfg == 0, parts[0], parts[1])
+    far = jnp.where(cfg == 0, parts[2], parts[3])
+    each = PLANES * 2
+    base = core * RING * each
+    own = base + seq // 2
+    tiles[own] = near + pltpu.roll(far, CH, 1)
+
+    send(tiles.at[own], tiles.at[own], x_sem, across)
+    arrived(tiles.at[base + y * each + 2 * z + 1 - xh], x_sem)
+    both = tiles.at[pl.ds(base + y * each + 2 * z, 2)]
+    for d, where in enumerate(planes):
+        send(both, both, z_sem.at[d], where)
+    for d in range(1, PLANES):
+        z_at = lax.rem(z - d + PLANES, PLANES)
+        arrived(tiles.at[pl.ds(base + y * each + 2 * z_at, 2)], z_sem.at[d - 1])
+    plane = tiles.at[pl.ds(base + y * each, each)]
+    for d in (2, 1, 3):
+        send(plane, plane, y_sem.at[d], beside(1, d))
+    send(plane, plane, core_sem.at[0], partner)
+    for d in (1, 3, 2):
+        y_at = lax.rem(y - d + RING, RING)
+        plane = tiles.at[pl.ds(base + y_at * each, each)]
+        arrived(plane, y_sem.at[d])
+        send(plane, plane, core_sem.at[d], partner)
+    for d in range(RING):
+        y_at = lax.rem(y - d + RING, RING)
+        arrived(tiles.at[pl.ds((1 - core) * RING * each + y_at * each, each)], core_sem.at[d])
+
+    tile = text_slots // (2 * PART) + tile_ref[0]
+    first = tile * 2 * PART + PART * cfg
+
+    def held(block):
+        got = tiles[lax.rem(block, 2) * RING * each + block // 2]
+        late = tile - rows * block // (2 * PART)
+        return jnp.where(late == 0, got, pltpu.roll(got, CH, 1))
+
+    begin = first // rows
+    end = (first + PART - 1) // rows
+    picked = held(begin)
+    picked += jnp.where(end == begin, jnp.zeros_like(picked), held(end))
+    mine_ref[...] = picked[:, :CH]
 
     for copy in sent:
         copy.wait_send()
@@ -338,13 +394,14 @@
     vmem = pl.BlockSpec(memory_space=pltpu.VMEM)
     bf16, f32 = jnp.bfloat16, jnp.float32
     dma = pltpu.SemaphoreType.DMA
-    stream, guided = pl.pallas_call(
+    tile = jnp.sum(jnp.where(owner == myself, jnp.arange(nseq, dtype=jnp.int32), 0))
+    stream, mine = pl.pallas_call(
         functools.partial(attention_kernel, textslots),
         out_shape=(
             jax.ShapeDtypeStruct(residual.shape[1:], bf16),
-            jax.ShapeDtypeStruct((tokens, CH), f32),
+            jax.ShapeDtypeStruct((PART, CH), f32),
         ),
-        in_specs=[pl.BlockSpec(memory_space=pltpu.SMEM)]
+        in_specs=[pl.BlockSpec(memory_space=pltpu.SMEM)] * 2
         + [vmem] * 5
         + [pl.BlockSpec(memory_space=pl.ANY), vmem],
         out_specs=(vmem, vmem),
@@ -366,8 +423,10 @@
             pltpu.VMEM((tokens, width), bf16),
             pltpu.VMEM((tokens, CH), f32),
             pltpu.VMEM((tokens, CH), f32),
+            pltpu.VMEM((4 * PART, 2 * CH), f32),
+            pltpu.VMEM((nseq, PART, 2 * CH), f32),
             dma,
-            dma((73,)),
+            dma((88,)),
             dma((4, RING)),
             dma((20,)),
             dma((len(ORDER), 2)),
@@ -376,19 +435,16 @@
             dma((len(ORDER),)),
             dma((GROUPS,)),
             dma,
+            dma,
+            dma((PLANES - 1,)),
+            dma((RING,)),
+            dma((RING,)),
         ],
         compiler_params=pltpu.CompilerParams(
             collective_id=0, has_side_effects=True, vmem_limit_bytes=60 * 1024 * 1024
         ),
-    )(text_len, queries[0], keys[0], values[0], residual[0], gate, w_out, w_final)
-    gathered = lax.all_gather(guided, "seq", axis=0, tiled=True)
-    columns = latent.shape[1]
-    tilerows = columns * lax.axis_size("cfg") // CH
-    mytile = jnp.sum(jnp.where(owner == myself, jnp.arange(nseq, dtype=jnp.int32), 0))
-    picked = lax.dynamic_slice_in_dim(gathered, textslots + mytile * tilerows, tilerows, 0)
-    flat = picked.reshape(tilerows * CH)
-    mine = lax.dynamic_slice_in_dim(flat, lax.axis_index("cfg") * columns, columns, 0)
-    latent_next = latent - 0.25 * mine.reshape(1, columns)
+    )(text_len, tile.reshape(1), queries[0], keys[0], values[0], residual[0], gate, w_out, w_final)
+    latent_next = latent - 0.25 * mine.reshape(latent.shape)
     return (stream[None], latent_next)
 
 

time: 197 us -> 88.1 us (0.45)
  waiting for transfers between devices: 116 us -> 0 us
  Pallas kernels: 58.9 us -> 80.1 us
  between operations: 15.4 us -> 1.31 us
    all_gather x1 -> x0, waiting for transfers between devices: 116 us -> none  [local(): gathered = lax.all_gather(guided, 'seq', axis=0, tiled=True)]
    pallas_call x1, Pallas kernels: 58.9 us -> 80.1 us  [local(): pl.pallas_call(functools.partial(attention_kernel, textslots), out_shape=...]
    unnamed x9 -> x4, local copies, waits for them, and re-layouts: 5.31 us -> 3.81 us
  transfers between devices with their start and end apart: 1 -> 0, of which waited for: 1 -> 0; matrix products, arithmetic and copies ran while one was open for 0% -> 0% of each run, Pallas kernels for 0% -> 0%
where the time goes in v3:
time: 88.1 us; the launch traced here: 87.9 us
  Pallas kernels  80.1 us (91%)
  local copies, waits for them, and re-layouts  3.89 us (4%)
  other arithmetic  2.59 us (3%)
  between operations  1.31 us (1%)
    pallas_call x1, Pallas kernels, local(): pl.pallas_call(functools.partial(attention_kernel, textslots), out_shape=...  80.1 us
    unnamed x4, local copies, waits for them, and re-layouts  3.81 us

profile of v3, /device:TPU:1, one launch (start us, length us, event | category | flops | bytes accessed | tf_op | source)
XLA Modules:
  0.0 87.9 jit_solution(5776771179711887802)
XLA Ops:
  0.6 0.0 copy-start
  1.3 1.3 %fusion = s32[]{:T(128)} fusion(s32[128]{0:T(128)} %param.19, s32[]{:T(128)S(6)} %axis_index.12), kind=kLoop, calls=%fused_computation.2 | loop fusion | flops 383 | bytes 520 | tf_op jit(solution)/shard_map/reduce_sum | solution.py:397
  2.6 2.1 %copy.12.w_final_ref = bf16[3072,64]{1,0:T(8,128)(2,1)} copy(bf16[3072,64]{0,1:T(8,128)(2,1)} %param.17) | data formatting | bytes 786432 | tf_op args[7]
  4.7 80.1 %shard_map.113 = (bf16[36,3072]{1,0:T(8,128)(2,1)}, f32[16,64]{1,0:T(8,128)}) custom-call(s32[1]{0:T(128)S(6)} %copy.14.limit_ref, s32[1]{0:T(128)} %bitcast.tile_ref, bf16[36,1536]{1,0:T(8,128)(2,1)} %bitcast.8, bf16[36,1536]{1,0:T(8,128)(2,1)} %bitcast.9, bf16[36,1536]{1,0:T(8,128)(2,1)} %bitcast.10, bf16[36,3072]{1,0:T(8,128)(2,1)} %bitcast.7, ...), custom_call_target="tpu_custom_call" | custom-call | tf_op jit(solution)/shard_map/pallas_call | solution.py:398
  84.8 0.7 broadcast_multiply_fusion
  85.5 0.1 mul.19
  85.6 0.0 copy-done
  85.6 0.6 sub.3
  86.2 1.7 %copy.15 = bf16[1,36,3072]{2,1,0:T(8,128)(2,1)} copy(bf16[1,36,3072]{2,1,0:T(8,128)(2,1)} %bitcast.6) | data formatting | bytes 442368
Async XLA Ops:
  0.6 85.0 %copy-start = (f32[1,1024]{1,0:T(1,128)S(1)}, f32[1,1024]{1,0:T(1,128)}, u32[]{:S(2)}) copy-start(f32[1,1024]{1,0:T(1,128)} %param.18) | copy-start | bytes 12292

commit v4 on v3

--- a/solution.py
+++ b/solution.py
@@ -30,7 +30,7 @@
 def attention_kernel(
     text_slots,
     limit_ref,
-    tile_ref,
+    owner_ref,
     q_ref,
     k_ref,
     v_ref,
@@ -38,8 +38,9 @@
     gate_ref,
     w_out_ref,
     w_final_ref,
+    latent_ref,
     hidden_ref,
-    mine_ref,
+    latent_next_ref,
     w_out,
     limit_own,
     limit_in,
@@ -311,7 +312,7 @@
     for g in range(GROUPS):
         arrived(attn.at[:, pl.ds(g * cols, cols)], o_sem.at[g])
 
-    width = hidden_ref.shape[1]
+    width = hidden_ref.shape[2]
     step = 512
     rate = jnp.zeros(speed.shape, jnp.float32)
     for at in range(0, width, step):
@@ -319,8 +320,13 @@
         proj = jnp.dot(attn[...], w_out[:, lanes], preferred_element_type=jnp.float32)
         stream = residual_ref[:, lanes].astype(jnp.float32) + gate_ref[:, lanes] * proj
         stream = stream.astype(jnp.bfloat16)
-        hidden_ref[:, lanes] = stream
-        rate += jnp.dot(stream, w_final_ref[lanes, :], preferred_element_type=jnp.float32)
+        hidden_ref[0, :, lanes] = stream
+        rate += lax.dot_general(
+            stream,
+            w_final_ref[:, lanes],
+            (((1,), (1,)), ((), ())),
+            preferred_element_type=jnp.float32,
+        )
     speed[...] = rate
     to = device(2 * xh + 1 - cfg, y, z, core)
     send(speed, speed_in, speed_sem, to)
@@ -337,7 +343,7 @@
     each = PLANES * 2
     base = core * RING * each
     own = base + seq // 2
-    tiles[own] = near + pltpu.roll(far, CH, 1)
+    tiles[own] = (near + pltpu.roll(far, CH, 1)).astype(jnp.bfloat16)
 
     send(tiles.at[own], tiles.at[own], x_sem, across)
     arrived(tiles.at[base + y * each + 2 * z + 1 - xh], x_sem)
@@ -360,11 +366,14 @@
         y_at = lax.rem(y - d + RING, RING)
         arrived(tiles.at[pl.ds((1 - core) * RING * each + y_at * each, each)], core_sem.at[d])
 
-    tile = text_slots // (2 * PART) + tile_ref[0]
+    found = jnp.int32(0)
+    for i in range(owner_ref.shape[0]):
+        found = jnp.where(owner_ref[i] == seq, i, found)
+    tile = text_slots // (2 * PART) + found
     first = tile * 2 * PART + PART * cfg
 
     def held(block):
-        got = tiles[lax.rem(block, 2) * RING * each + block // 2]
+        got = tiles[lax.rem(block, 2) * RING * each + block // 2].astype(jnp.float32)
         late = tile - rows * block // (2 * PART)
         return jnp.where(late == 0, got, pltpu.roll(got, CH, 1))
 
@@ -372,7 +381,10 @@
     end = (first + PART - 1) // rows
     picked = held(begin)
     picked += jnp.where(end == begin, jnp.zeros_like(picked), held(end))
-    mine_ref[...] = picked[:, :CH]
+    for i in range(PART // 2):
+        lanes = slice(2 * CH * i, 2 * CH * (i + 1))
+        pair = [picked[2 * i + r : 2 * i + r + 1, :CH] for r in range(2)]
+        latent_next_ref[:, lanes] = latent_ref[:, lanes] - 0.25 * jnp.concatenate(pair, axis=1)
 
     for copy in sent:
         copy.wait_send()
@@ -386,7 +398,6 @@
 def local(queries, keys, values, residual, gate, text_len, w_out, w_final, latent, owner):
     tokens, width = queries.shape[1:]
     nseq = lax.axis_size("seq")
-    myself = lax.axis_index("seq")
     seqlen = tokens * nseq
     textslots = seqlen // 9
     cols = MINE * HEAD
@@ -394,16 +405,15 @@
     vmem = pl.BlockSpec(memory_space=pltpu.VMEM)
     bf16, f32 = jnp.bfloat16, jnp.float32
     dma = pltpu.SemaphoreType.DMA
-    tile = jnp.sum(jnp.where(owner == myself, jnp.arange(nseq, dtype=jnp.int32), 0))
-    stream, mine = pl.pallas_call(
+    return pl.pallas_call(
         functools.partial(attention_kernel, textslots),
         out_shape=(
-            jax.ShapeDtypeStruct(residual.shape[1:], bf16),
-            jax.ShapeDtypeStruct((PART, CH), f32),
+            jax.ShapeDtypeStruct(residual.shape, bf16),
+            jax.ShapeDtypeStruct(latent.shape, f32),
         ),
         in_specs=[pl.BlockSpec(memory_space=pltpu.SMEM)] * 2
         + [vmem] * 5
-        + [pl.BlockSpec(memory_space=pl.ANY), vmem],
+        + [pl.BlockSpec(memory_space=pl.ANY), vmem, vmem],
         out_specs=(vmem, vmem),
         scratch_shapes=[
             pltpu.VMEM(w_out.shape, bf16),
@@ -424,7 +434,7 @@
             pltpu.VMEM((tokens, CH), f32),
             pltpu.VMEM((tokens, CH), f32),
             pltpu.VMEM((4 * PART, 2 * CH), f32),
-            pltpu.VMEM((nseq, PART, 2 * CH), f32),
+            pltpu.VMEM((nseq, PART, 2 * CH), bf16),
             dma,
             dma((88,)),
             dma((4, RING)),
@@ -443,9 +453,7 @@
         compiler_params=pltpu.CompilerParams(
             collective_id=0, has_side_effects=True, vmem_limit_bytes=60 * 1024 * 1024
         ),
-    )(text_len, tile.reshape(1), queries[0], keys[0], values[0], residual[0], gate, w_out, w_final)
-    latent_next = latent - 0.25 * mine.reshape(latent.shape)
-    return (stream[None], latent_next)
+    )(text_len, owner, queries[0], keys[0], values[0], residual[0], gate, w_out, w_final.T, latent)
 
 
 def solution(mesh):

time: 88.1 us -> 81.9 us (0.930)
  Pallas kernels: 80.1 us -> 77.5 us
  other arithmetic: 2.59 us -> 0 us
  local copies, waits for them, and re-layouts: 3.89 us -> 2.92 us
    pallas_call x1, Pallas kernels: 80.1 us -> 77.5 us  [local(): pl.pallas_call(functools.partial(attention_kernel, textslots), out_shape=...]
    reduce_sum x1 -> x0, other arithmetic: 1.29 us -> none  [local(): jnp.sum(jnp.where(owner == myself, jnp.arange(nseq, dtype=jnp.int32), 0))]
    unnamed x4 -> x2, local copies, waits for them, and re-layouts: 3.81 us -> 2.92 us
where the time goes in v4:
time: 81.9 us; the launch traced here: 81.7 us
  Pallas kernels  77.5 us (95%)
  local copies, waits for them, and re-layouts  2.92 us (4%)
  between operations  1.29 us (2%)
    pallas_call x1, Pallas kernels, local(): pl.pallas_call(functools.partial(attention_kernel, textslots), out_shape=...  77.5 us
    unnamed x2, local copies, waits for them, and re-layouts  2.92 us

profile of v4, /device:TPU:1, one launch (start us, length us, event | category | flops | bytes accessed | tf_op | source)
XLA Modules:
  0.0 81.7 jit_solution(8001156654936736068)
XLA Ops:
  1.3 77.5 %shard_map.113 = (bf16[1,36,3072]{2,1,0:T(8,128)(2,1)}, f32[1,1024]{1,0:T(1,128)}) custom-call(s32[1]{0:T(128)S(6)} %copy.14.limit_ref, s32[128]{0:T(128)} %owner_ref.1, bf16[36,1536]{1,0:T(8,128)(2,1)} %bitcast.7, bf16[36,1536]{1,0:T(8,128)(2,1)} %bitcast.8, bf16[36,1536]{1,0:T(8,128)(2,1)} %bitcast.9, bf16[36,3072]{1,0:T(8,128)(2,1)} %bitcast.6, ...), custom_call_target="tpu_custom_call" | custom-call | tf_op jit(solution)/shard_map/pallas_call | solution.py:408
  78.8 1.7 %copy.15 = bf16[1,36,3072]{2,1,0:T(8,128)(2,1)} copy(bf16[1,36,3072]{2,1,0:T(8,128)(2,1)} %get-tuple-element.4) | data formatting | bytes 442368
  80.5 1.3 %copy.16 = f32[1,1024]{1,0:T(1,128)} copy(f32[1,1024]{1,0:T(1,128)} %get-tuple-element.5) | data formatting | bytes 8192
